TPU v7x, 32 devices: a whole 2x2x4 slice. The times are simulated.
32 devices in a mesh: groups: 2 (over x), chan: 16 (over z, y, core).
Axes of the slice: x: 2, y: 2, z: 4, core: 2. Of those that a mesh axis runs over, the one named last changes fastest.
Arguments:
- data: bfloat16 [28672, 4096], P(('groups', 'chan')), parts along dimension 0, as said below
- alive: int32 [8192], P(('groups', 'chan')), parts along dimension 0, may hold values 0 or 1
- sources: int32 [2, 16], replicated, may hold values from 0 to 4095, as said below
Outputs:
- correlations: bfloat16 [4, 16, 256, 4096], P('groups', None, None, 'chan'), parts along dimension 0
There are 2 independent parts, one for each index of `groups`. A program takes and returns all parts, laid end to end along the dimension named above; an argument that names none is the same for every part. Nothing has to cross between parts.
Inputs may be any that keep to these rules, and one draw needn't show every extreme that they name: `sources`: no channel number appears twice in the array, and channel 4096 - 1 is always one of them. `data`: samples have channel and time-block scales of their own.
All inputs are finite; a program needn't handle non-finite values. No bound on the sum of `alive` on one device may be relied on, other than what follows from the above.
Results may differ from a plain program's by a relative error of at most 0.0076.
Values may be sent and summed in bfloat16 or wider, within the bound.
No kernel may reach another device: no remote copies, remote signals or barrier semaphores. Data moves between devices by JAX's collectives and lax.ppermute only.
A program may use at most 128 MiB of HBM per device.

v0:
```python
import math
import jax
import jax.numpy as jnp
from jax import lax
from jax.sharding import PartitionSpec as P

SEGMENT_LENGTH = 512
NF = 128
LAGS = 256
SRC = 16
ROUNDS = 2
SEGMENT_TALLY = 28


def forward_table():
    times = jnp.arange(SEGMENT_LENGTH, dtype=jnp.int32)[:, None]
    bins = jnp.arange(NF, dtype=jnp.int32)[None, :] + 1
    angle = 2.0 * math.pi / SEGMENT_LENGTH * (bins * times % SEGMENT_LENGTH).astype(jnp.float32)
    table = jnp.concatenate([jnp.cos(angle), -jnp.sin(angle)], axis=1) / math.sqrt(SEGMENT_LENGTH)
    return table.astype(jnp.bfloat16)


def inverse_table():
    shifts = jnp.arange(LAGS, dtype=jnp.int32)[:, None] - LAGS // 2
    bins = jnp.arange(NF, dtype=jnp.int32)[None, :] + 1
    angle = 2.0 * math.pi / SEGMENT_LENGTH * (bins * shifts % SEGMENT_LENGTH).astype(jnp.float32)
    return jnp.concatenate([jnp.cos(angle), -jnp.sin(angle)], axis=1).astype(jnp.bfloat16)


def body(data, alive, sources):
    count = lax.axis_size("chan")
    width = data.shape[1] // count
    table = forward_table()
    split = data.reshape(data.shape[0], count, width)
    moved = lax.all_to_all(split, "chan", split_axis=1, concat_axis=0, tiled=True)
    blocks = moved.reshape(SEGMENT_TALLY, SEGMENT_LENGTH, moved.shape[2])
    spectra = jnp.einsum("tk,wtc->wkc", table, blocks, preferred_element_type=jnp.float32)
    level = jnp.mean(spectra[:, :NF] ** 2 + spectra[:, NF:] ** 2, axis=0)
    factor = alive.astype(jnp.float32)[None, :] / jnp.sqrt(level + 0.01)
    factor = jnp.concatenate([factor, factor], axis=0)
    whitened = (spectra * factor[None]).astype(jnp.bfloat16)
    ids = sources.reshape(-1)
    owner = ids // width
    local = ids % width
    mine = owner == lax.axis_index("chan")
    picked = jnp.transpose(jnp.take(whitened, local, axis=2), (2, 0, 1)).astype(jnp.float32)
    picked = jnp.where(mine[:, None, None], picked, 0.0)
    src = lax.psum(picked, "chan").astype(jnp.bfloat16)
    src_re, src_im = (src[:, :, :NF], src[:, :, NF:])
    own_re, own_im = (whitened[:, :NF], whitened[:, NF:])
    form = "qwf,wfc->qfc"
    correlogram_realpart = jnp.einsum(
        form, src_re, own_re, preferred_element_type=jnp.float32
    ) + jnp.einsum(form, src_im, own_im, preferred_element_type=jnp.float32)
    cross_imaginary = jnp.einsum(
        form, src_re, own_im, preferred_element_type=jnp.float32
    ) - jnp.einsum(form, src_im, own_re, preferred_element_type=jnp.float32)
    cross = jnp.concatenate([correlogram_realpart, cross_imaginary], axis=1).astype(jnp.bfloat16)
    lagged = jnp.einsum("lk,qkc->qlc", inverse_table(), cross, preferred_element_type=jnp.float32)
    lagged = lagged / math.sqrt(NF * SEGMENT_TALLY)
    return lagged.reshape(ROUNDS, SRC, LAGS, width).astype(jnp.bfloat16)


def solution(mesh):
    return jax.shard_map(
        body,
        mesh=mesh,
        in_specs=(P(("groups", "chan"), None), P(("groups", "chan")), P()),
        out_specs=P("groups", None, None, "chan"),
        check_vma=False,
    )
```

profile of v0, /device:TPU:0, one launch (start us, length us, event | category | flops | bytes accessed | tf_op | source)
XLA Modules:
  0.0 326.9 jit_solution(7985542122648060904)
XLA Ops:
  0.0 6.9 %copy.27 = bf16[112,16,8,256]{3,2,0,1:T(8,128)(2,1)} copy(bf16[112,16,8,256]{3,2,1,0:T(8,128)(2,1)} %bitcast.32) | data formatting | bytes 14680064 | tf_op jit(solution)/shard_map/reshape | solution.py:34
  6.9 0.0 copy-start.3
  6.9 0.0 copy-start.2
  6.9 7.6 %all-to-all-start = ((bf16[896,16,256]{2,0,1:T(8,128)(2,1)}), bf16[896,16,256]{2,0,1:T(8,128)(2,1)}, u32[]{:S(2)}, u32[]{:S(2)}) async-start(bf16[896,16,256]{2,0,1:T(8,128)(2,1)} %bitcast.31), calls=%async_computation | async-start | bytes 14680064 | tf_op jit(solution)/shard_map/all_to_all | solution.py:35
  14.4 0.0 copy-done.3
  14.4 0.1 reshape.125
  14.5 0.1 reshape.124
  14.6 0.0 copy-done.2
  14.7 0.6 cosine_convert_fusion
  15.3 1.1 fusion.33
  16.4 130.5 %all-to-all-done = bf16[896,16,256]{2,0,1:T(8,128)(2,1)} async-done(((bf16[896,16,256]{2,0,1:T(8,128)(2,1)}), bf16[896,16,256]{2,0,1:T(8,128)(2,1)}, u32[]{:S(2)}, u32[]{:S(2)}) %all-to-all-start) | async-done | bytes 7340064 | tf_op jit(solution)/shard_map/all_to_all | solution.py:35
  146.9 5.2 %convolution_bitcast_fusion = f32[28,256,256]{2,1,0:T(8,128)S(1)} fusion(bf16[28,512,256]{2,1,0:T(8,128)(2,1)} %bitcast.3, f32[512,128]{0,1:T(8,128)S(1)} %get-tuple-element.14, f32[512,128]{0,1:T(8,128)S(1)} %get-tuple-element.13), kind=kOutput, calls=%fused_computation.14 | convolution fusion | flops 1879441408 | bytes 15204352 | tf_op jit(solution)/shard_map/tk,wtc->wkc/dot_general | solution.py:37
  152.0 0.5 fusion.5
  152.6 2.6 multiply_convert_fusion.1
  155.2 7.7 %copy.7 = bf16[28,256,256]{1,0,2:T(8,128)(2,1)} copy(bf16[28,256,256]{2,1,0:T(8,128)(2,1)} %multiply_convert_fusion.1) | data formatting | bytes 7340032 | tf_op jit(solution)/shard_map/convert_element_type | solution.py:41
  162.9 3.6 %fusion.40 = (bf16[28,128,256]{2,1,0:T(8,128)(2,1)S(1)}, bf16[28,128,256]{2,1,0:T(8,128)(2,1)}) fusion(bf16[28,256,256]{2,1,0:T(8,128)(2,1)} %multiply_convert_fusion.1), kind=kLoop, calls=%fused_computation.76 | loop fusion | bytes 7340032 | tf_op jit(solution)/shard_map/slice | solution.py:50
  166.6 2.8 gather_fusion
  169.3 0.2 convert_select_fusion
  169.6 100.6 %all-reduce.1 = bf16[32,28,256]{2,1,0:T(8,128)(2,1)S(1)} all-reduce(f32[32,28,256]{2,1,0:T(8,128)S(1)} %convert_select_fusion), channel_id=1, replica_groups=mesh['groups'=2,'chan'=16] {'chan'}, use_global_device_ids=true, to_apply=%region_1.2 | all-reduce | flops 229376 | bytes 1376256 | tf_op jit(solution)/shard_map/psum | solution.py:48
  270.2 0.1 fusion.41
  270.3 2.6 copy.13
  272.8 1.6 copy.10
  274.5 0.0 copy-start
  274.5 0.0 copy-start.1
  274.5 4.6 %fusion.14 = f32[128,256,32]{1,2,0:T(8,128)} fusion(bf16[32,28,128]{0,1,2:T(8,128)(2,1)} %copy.13, bf16[28,128,256]{2,1,0:T(8,128)(2,1)S(1)} %get-tuple-element.5), kind=kOutput, calls=%fused_computation.21 | convolution fusion | flops 58720256 | bytes 6258688 | tf_op jit(solution)/shard_map/qwf,wfc->qfc/dot_general | solution.py:57
  279.1 0.0 copy-done
  279.1 0.0 copy-done.1
  279.1 3.2 fusion.12
  282.4 3.3 fusion.10
  285.6 3.3 %fusion.16 = f32[128,256,32]{1,2,0:T(8,128)} fusion(bf16[32,28,128]{0,1,2:T(8,128)(2,1)S(1)} %copy.10, bf16[28,128,256]{2,1,0:T(8,128)(2,1)S(1)} %get-tuple-element.5), kind=kOutput, calls=%fused_computation.23 | convolution fusion | flops 58720256 | bytes 6258688 | tf_op jit(solution)/shard_map/qwf,wfc->qfc/dot_general | solution.py:52
  288.9 5.3 %copy.16 = f32[128,256,32]{0,1,2:T(8,128)} copy(f32[128,256,32]{1,2,0:T(8,128)} %fusion.14) | data formatting | bytes 8388608 | tf_op jit(solution)/shard_map/qwf,wfc->qfc/dot_general | solution.py:57
  294.2 5.3 %copy.15 = f32[128,256,32]{0,1,2:T(8,128)} copy(f32[128,256,32]{1,2,0:T(8,128)} %fusion.10) | data formatting | bytes 8388608 | tf_op jit(solution)/shard_map/qwf,wfc->qfc/dot_general | solution.py:55
  299.6 5.3 %copy.14 = f32[128,256,32]{0,1,2:T(8,128)} copy(f32[128,256,32]{1,2,0:T(8,128)} %fusion.12) | data formatting | bytes 8388608 | tf_op jit(solution)/shard_map/qwf,wfc->qfc/dot_general | solution.py:54
  304.9 5.3 %copy.11 = f32[128,256,32]{0,1,2:T(8,128)} copy(f32[128,256,32]{1,2,0:T(8,128)} %fusion.16) | data formatting | bytes 8388608 | tf_op jit(solution)/shard_map/qwf,wfc->qfc/dot_general | solution.py:52
  310.2 7.6 %fusion.8 = (bf16[32,128,256]{1,2,0:T(8,128)(2,1)S(1)}, bf16[32,128,256]{1,2,0:T(8,128)(2,1)S(1)}) fusion(f32[128,256,32]{0,1,2:T(8,128)} %copy.11, f32[128,256,32]{0,1,2:T(8,128)} %copy.14, f32[128,256,32]{0,1,2:T(8,128)} %copy.15, f32[128,256,32]{0,1,2:T(8,128)} %copy.16), kind=kLoop, calls=%fused_computation.15 | loop fusion | flops 4194304 | bytes 20971520 | tf_op jit(solution)/shard_map/add | solution.py:52
  317.8 2.9 multiply_convert_fusion
  320.7 6.2 %copy.8 = bf16[2,16,256,256]{3,2,1,0:T(8,128)(2,1)} copy(bf16[2,16,256,256]{2,3,1,0:T(8,128)(2,1)} %bitcast.33) | data formatting | bytes 8388608 | tf_op jit(solution)/shard_map/convert_element_type | solution.py:61
  (8 shorter events, 0.1 us)
Async XLA Ops:
  6.9 7.6 %copy-start.3 = (s32[2,16]{1,0:T(2,128)S(1)}, s32[2,16]{1,0:T(2,128)}, u32[]{:S(2)}) copy-start(s32[2,16]{1,0:T(2,128)} %param.5) | copy-start | bytes 388
  6.9 7.8 %copy-start.2 = (s32[256]{0:T(256)S(1)}, s32[256]{0:T(256)}, u32[]{:S(2)}) copy-start(s32[256]{0:T(256)} %param.4) | copy-start | bytes 3076
  6.9 140.0 %all-to-all-start = ((bf16[896,16,256]{2,0,1:T(8,128)(2,1)}), bf16[896,16,256]{2,0,1:T(8,128)(2,1)}, u32[]{:S(2)}, u32[]{:S(2)}) async-start(bf16[896,16,256]{2,0,1:T(8,128)(2,1)} %bitcast.31), calls=%async_computation | async-start | bytes 14680064 | tf_op jit(solution)/shard_map/all_to_all | solution.py:35
  274.5 4.7 %copy-start = (bf16[28,128,256]{2,1,0:T(8,128)(2,1)S(1)}, bf16[28,128,256]{2,1,0:T(8,128)(2,1)}, u32[]{:S(2)}) copy-start(bf16[28,128,256]{2,1,0:T(8,128)(2,1)} %get-tuple-element.6) | copy-start | bytes 5505028
  274.5 4.7 %copy-start.1 = (bf16[32,28,128]{0,1,2:T(8,128)(2,1)S(1)}, bf16[32,28,128]{0,1,2:T(8,128)(2,1)}, u32[]{:S(2)}) copy-start(bf16[32,28,128]{0,1,2:T(8,128)(2,1)} %copy.13) | copy-start | bytes 688132
where the time goes:
time: 328 us; the launch traced here: 327 us
  waiting for transfers between devices  130 us (40%)
  blocking collectives  101 us (31%)
  local copies, waits for them, and re-layouts  52.9 us (16%)
  matrix products  22.5 us (7%)
  other arithmetic  12.8 us (4%)
  starting transfers between devices  7.56 us (2%)
    all_to_all x1, waiting for transfers between devices, body(): lax.all_to_all(split, 'chan', split_axis=1, concat_axis=0, tiled=True)  130 us
    psum x1, blocking collectives, body(): src = lax.psum(picked, 'chan').astype(jnp.bfloat16)  101 us
    convert_element_type x1, local copies, waits for them, and re-layouts, body(): whitened = (spectra * factor[None]).astype(jnp.bfloat16)  7.7 us
    add x1, other arithmetic, body(): jnp.einsum(form, src_re, own_re, preferred_element_type=jnp.float32)  7.63 us
    all_to_all x1, starting transfers between devices, body(): lax.all_to_all(split, 'chan', split_axis=1, concat_axis=0, tiled=True)  7.56 us
    reshape x1, local copies, waits for them, and re-layouts, body(): split = data.reshape(data.shape[0], count, width)  6.85 us
  transfers between devices with their start and end apart: 1, of which 1 were waited for; matrix products, arithmetic and copies ran while one was open for 1% of the time, Pallas kernels for 0%

commit v1 on v0

--- a/solution.py
+++ b/solution.py
@@ -45,7 +45,7 @@
     mine = owner == lax.axis_index("chan")
     picked = jnp.transpose(jnp.take(whitened, local, axis=2), (2, 0, 1)).astype(jnp.float32)
     picked = jnp.where(mine[:, None, None], picked, 0.0)
-    src = lax.psum(picked, "chan").astype(jnp.bfloat16)
+    src = jnp.sum(lax.all_gather(picked, "chan"), axis=0).astype(jnp.bfloat16)
     src_re, src_im = (src[:, :, :NF], src[:, :, NF:])
     own_re, own_im = (whitened[:, :NF], whitened[:, NF:])
     form = "qwf,wfc->qfc"

time: 328 us -> 354 us (1.079)
  waiting for transfers between devices: 130 us -> 268 us
  blocking collectives: 101 us -> 0 us
  local copies, waits for them, and re-layouts: 52.9 us -> 32.7 us
  between operations: 0.16 us -> 13.5 us
    all_gather x0 -> x1, waiting for transfers between devices: none -> 137 us  [body(): src = jnp.sum(lax.all_gather(picked, 'chan'), axis=0).astype(jnp.bfloat16)]
    psum x1 -> x0, blocking collectives: 101 us -> none  [body(): src = lax.psum(picked, 'chan').astype(jnp.bfloat16)]
    dot_general x4 -> x0, local copies, waits for them, and re-layouts: 21.3 us -> none  [the longest x1 5.34 us: body(): jnp.einsum(form, src_re, own_im, preferred_element_type=jnp.float32)]
    add x1 -> x0, other arithmetic: 7.63 us -> none  [body(): jnp.einsum(form, src_re, own_re, preferred_element_type=jnp.float32)]
    reduce_sum x0 -> x1, other arithmetic: none -> 7.04 us  [body(): src = jnp.sum(lax.all_gather(picked, 'chan'), axis=0).astype(jnp.bfloat16)]
    dot_general x1, matrix products: 2.88 us -> 7.24 us  [body(): jnp.einsum('lk,qkc->qlc', inverse_table(), cross, preferred_element_type=...]
    slice x3 -> x0, local copies, waits for them, and re-layouts: 4.28 us -> none  [body(): src_re, src_im = (src[:, :, :NF], src[:, :, NF:])]
    reduce_sum x0 -> x1, local copies, waits for them, and re-layouts: none -> 4 us  [body(): src = jnp.sum(lax.all_gather(picked, 'chan'), axis=0).astype(jnp.bfloat16)]
  transfers between devices with their start and end apart: 1 -> 2, of which waited for: 1 -> 2; matrix products, arithmetic and copies ran while one was open for 1% -> 2% of each run, Pallas kernels for 0% -> 0%
where the time goes in v1:
time: 354 us
  waiting for transfers between devices  268 us (76%)
  local copies, waits for them, and re-layouts  32.7 us (9%)
  matrix products  19 us (5%)
  between operations  13.5 us (4%)
  other arithmetic  12.5 us (4%)
  starting transfers between devices  7.6 us (2%)
    all_gather x1, waiting for transfers between devices, body(): src = jnp.sum(lax.all_gather(picked, 'chan'), axis=0).astype(jnp.bfloat16)  137 us
    all_to_all x1, waiting for transfers between devices, body(): lax.all_to_all(split, 'chan', split_axis=1, concat_axis=0, tiled=True)  131 us
    convert_element_type x1, local copies, waits for them, and re-layouts, body(): whitened = (spectra * factor[None]).astype(jnp.bfloat16)  7.7 us
    all_to_all x1, starting transfers between devices, body(): lax.all_to_all(split, 'chan', split_axis=1, concat_axis=0, tiled=True)  7.56 us
    dot_general x1, matrix products, body(): jnp.einsum('lk,qkc->qlc', inverse_table(), cross, preferred_element_type=...  7.24 us
  transfers between devices with their start and end apart: 2, of which 2 were waited for; matrix products, arithmetic and copies ran while one was open for 2% of the time, Pallas kernels for 0%

profile of v1, /device:TPU:0, one launch (start us, length us, event | category | flops | bytes accessed | tf_op | source)
XLA Modules:
  0.0 353.8 jit_solution(13141758108189014661)
XLA Ops:
  6.5 6.8 %copy.38 = bf16[112,16,8,256]{3,2,0,1:T(8,128)(2,1)} copy(bf16[112,16,8,256]{3,2,1,0:T(8,128)(2,1)} %bitcast.30) | data formatting | bytes 14680064 | tf_op jit(solution)/shard_map/reshape | solution.py:34
  13.4 0.0 copy-start.3
  13.4 0.0 copy-start.2
  13.4 7.6 %all-to-all-start = ((bf16[896,16,256]{2,0,1:T(8,128)(2,1)}), bf16[896,16,256]{2,0,1:T(8,128)(2,1)}, u32[]{:S(2)}, u32[]{:S(2)}) async-start(bf16[896,16,256]{2,0,1:T(8,128)(2,1)} %bitcast.28), calls=%async_computation | async-start | bytes 14680064 | tf_op jit(solution)/shard_map/all_to_all | solution.py:35
  20.9 0.0 all-gather.3.cloned.1.call-start
  21.0 0.0 copy-done.3
  21.0 0.1 reshape.125
  21.1 0.1 reshape.124
  21.2 0.0 copy-done.2
  21.2 1.1 fusion.37
  22.3 131.1 %all-to-all-done = bf16[896,16,256]{2,0,1:T(8,128)(2,1)} async-done(((bf16[896,16,256]{2,0,1:T(8,128)(2,1)}), bf16[896,16,256]{2,0,1:T(8,128)(2,1)}, u32[]{:S(2)}, u32[]{:S(2)}) %all-to-all-start) | async-done | bytes 7340064 | tf_op jit(solution)/shard_map/all_to_all | solution.py:35
  153.4 5.2 %convolution_bitcast_fusion = f32[28,256,256]{2,1,0:T(8,128)S(1)} fusion(bf16[28,512,256]{2,1,0:T(8,128)(2,1)} %bitcast.3, f32[512,128]{0,1:T(8,128)S(1)} %get-tuple-element.12, f32[512,128]{0,1:T(8,128)S(1)} %get-tuple-element.11), kind=kOutput, calls=%fused_computation.13 | convolution fusion | flops 1879441408 | bytes 15204352 | tf_op jit(solution)/shard_map/tk,wtc->wkc/dot_general | solution.py:37
  158.5 0.5 fusion.3
  159.1 2.6 multiply_convert_fusion.1
  161.7 7.7 %copy.11 = bf16[28,256,256]{1,0,2:T(8,128)(2,1)} copy(bf16[28,256,256]{2,1,0:T(8,128)(2,1)} %multiply_convert_fusion.1) | data formatting | bytes 7340032 | tf_op jit(solution)/shard_map/convert_element_type | solution.py:41
  169.4 2.8 gather_fusion
  172.2 0.2 convert_select_fusion
  172.4 1.5 copy.12
  173.9 0.0 all-gather.3.cloned.1.call-update
  173.9 0.6 cosine_convert_fusion
  174.5 3.6 %fusion.44 = (bf16[28,128,256]{2,1,0:T(8,128)(2,1)S(1)}, bf16[28,128,256]{2,1,0:T(8,128)(2,1)}) fusion(bf16[28,256,256]{2,1,0:T(8,128)(2,1)} %multiply_convert_fusion.1), kind=kLoop, calls=%fused_computation.77 | loop fusion | bytes 7340032 | tf_op jit(solution)/shard_map/slice | solution.py:50
  178.2 137.4 %all-gather.3.cloned.1.call-done = f32[512,28,256]{2,0,1:T(8,128)} async-done(((f32[32,28,256]{2,0,1:T(8,128)}), f32[512,28,256]{2,0,1:T(8,128)}) %all-gather.3.cloned.1.call-update) | async-done | bytes 14680080 | tf_op jit(solution)/shard_map/all_gather | solution.py:48
  315.5 7.0 %reduce_sum.19 = bf16[32,28,256]{2,0,1:T(8,128)(2,1)S(1)} reduce(f32[16,32,28,256]{3,1,0,2:T(8,128)} %bitcast.29, f32[]{:T(128)} %constant.78.clone.1), dimensions={0}, to_apply=%region_1.2 | reduce | flops 3440640 | bytes 15138820 | tf_op jit(solution)/shard_map/reduce_sum | solution.py:48
  322.6 4.0 %copy.13 = bf16[32,28,256]{1,0,2:T(8,128)(2,1)} copy(bf16[32,28,256]{2,0,1:T(8,128)(2,1)S(1)} %reduce_sum.19) | data formatting | bytes 917504 | tf_op jit(solution)/shard_map/reduce_sum | solution.py:48
  326.6 0.0 copy-start
  326.6 0.0 copy-start.1
  326.6 2.6 fusion.10
  329.2 0.0 copy-done
  329.2 0.0 copy-done.1
  329.2 1.2 fusion.6
  330.4 1.3 fusion.12
  331.8 1.4 fusion.15
  333.2 0.4 pad_maximum_fusion
  333.6 7.2 %multiply_convert_fusion = bf16[32,256,256]{2,1,0:T(8,128)(2,1)} fusion(bf16[32,256,256]{2,0,1:T(8,128)(2,1)S(1)} %pad_maximum_fusion, bf16[256,128]{1,0:T(8,128)(2,1)S(1)} %get-tuple-element.8, bf16[256,128]{1,0:T(8,128)(2,1)S(1)} %get-tuple-element.7), kind=kOutput, calls=%fused_computation.1 | convolution fusion | flops 1078198272 | bytes 8519680 | tf_op jit(solution)/shard_map/lk,qkc->qlc/dot_general | solution.py:59
  340.8 6.2 %copy.19 = bf16[2,16,256,256]{3,2,1,0:T(8,128)(2,1)} copy(bf16[2,16,256,256]{2,3,1,0:T(8,128)(2,1)} %bitcast.31) | data formatting | bytes 8388608 | tf_op jit(solution)/shard_map/convert_element_type | solution.py:61
  (8 shorter events, 0.1 us)
Async XLA Ops:
  13.4 7.6 %copy-start.3 = (s32[2,16]{1,0:T(2,128)S(1)}, s32[2,16]{1,0:T(2,128)}, u32[]{:S(2)}) copy-start(s32[2,16]{1,0:T(2,128)} %param.5) | copy-start | bytes 388
  13.4 7.8 %copy-start.2 = (s32[256]{0:T(256)S(1)}, s32[256]{0:T(256)}, u32[]{:S(2)}) copy-start(s32[256]{0:T(256)} %param.4) | copy-start | bytes 3076
  13.4 140.0 %all-to-all-start = ((bf16[896,16,256]{2,0,1:T(8,128)(2,1)}), bf16[896,16,256]{2,0,1:T(8,128)(2,1)}, u32[]{:S(2)}, u32[]{:S(2)}) async-start(bf16[896,16,256]{2,0,1:T(8,128)(2,1)} %bitcast.28), calls=%async_computation | async-start | bytes 14680064 | tf_op jit(solution)/shard_map/all_to_all | solution.py:35
  20.9 294.6 %all-gather.3.cloned.1.call-start = ((), (), s32[]{:S(2)}) async-start(), calls=%async_computation.1 | async-start | bytes 15597568 | tf_op jit(solution)/shard_map/all_gather | solution.py:48
  326.6 2.6 copy-start
  326.6 2.6 copy-start.1
Sparse Core Ops, SparseCore 0:
  174.0 141.4 all-gather.2
